TPU v7x, 512 devices: a whole 4x8x8 slice. The times are simulated.
512 devices in a mesh: src: 128 (over y, z, core), depth: 4 (over x).
Axes of the slice: x: 4, y: 8, z: 8, core: 2. Of those that a mesh axis runs over, the one named last changes fastest.
Arguments:
- incident: float32 [128, 4, 2, 4096], P('src'), may hold values from -6 to 6
- encode: int32 [128], P('src'), may hold values from 0 to 15
- freq_index: int32 [128], P('src'), may hold values from 0 to 7
- wavenum: float32 [8], replicated, may hold values from 1 to 2.8
- slowness: float32 [4, 4096], P('depth'), may hold values from -6 to 6
- probes: bfloat16 [64, 4, 4096], P(None, 'depth'), may hold values from -6 to 6
Outputs:
- sketch_basis: float32 [64, 4, 4096], P(None, 'depth', 'src')
- r_factor: float32 [64, 64], replicated
All inputs are finite; a program needn't handle non-finite values.
Results may differ from a plain program's by a relative error of at most 0.02.
Values may be sent and summed in bfloat16 or wider, within the bound.
A program may use at most 128 MiB of HBM per device.

v0:
```python
import math
import jax
import jax.numpy as jnp
from jax import lax
from jax.sharding import Mesh, PartitionSpec as P

SIDE = 64
CHIPS_Y = 8
CHIPS_Z = 8
CORES = 2
SRC_AXES = ("chip_y", "chip_z", "core")
DAMPING = 0.5
STEP_DEPTH = 1.0


def dft_tables(points, direction):
    counter = jnp.arange(points, dtype=jnp.int32)
    product = counter[:, None] * counter[None, :] % points
    angles = 2.0 * math.pi / points * product.astype(jnp.float32)
    cosine = jnp.cos(angles) / math.sqrt(points)
    sine_part = direction * jnp.sin(angles) / math.sqrt(points)
    matrix = jnp.stack(
        [jnp.stack([cosine, sine_part], axis=1), jnp.stack([-sine_part, cosine], axis=1)], axis=0
    )
    matrix = matrix.astype(jnp.bfloat16)
    total_points = points * points
    twist_index = counter[:, None] * counter[None, :] % total_points
    twist_angle = 2.0 * math.pi / total_points * twist_index.astype(jnp.float32)
    return (matrix, jnp.cos(twist_angle), direction * jnp.sin(twist_angle))


def transform(values, tables):
    matrix, twist_real, twist_imag = tables
    points = matrix.shape[1]
    leading = values.shape[:-2]
    grid_values = values.reshape((-1, 2 * points, points))
    square = matrix.reshape(2 * points, 2 * points)
    segmented = jnp.einsum("nkb,km->nbm", grid_values, square, preferred_element_type=jnp.float32)
    real_part = segmented[:, :, :points]
    imag_part = segmented[:, :, points:]
    turned = jnp.concatenate(
        [
            real_part * twist_real - imag_part * twist_imag,
            real_part * twist_imag + imag_part * twist_real,
        ],
        axis=-1,
    )
    turned = turned.astype(jnp.bfloat16).reshape((-1, points, 2, points))
    result = jnp.einsum("nbsc,sbtd->ntdc", turned, matrix, preferred_element_type=jnp.float32)
    return result.reshape(leading + (2, points * points))


def complex_times(first, second):
    real_part = first[..., 0, :] * second[..., 0, :] - first[..., 1, :] * second[..., 1, :]
    imag_part = first[..., 0, :] * second[..., 1, :] + first[..., 1, :] * second[..., 0, :]
    return jnp.stack([real_part, imag_part], axis=-2)


def conjugate(values):
    return jnp.stack([values[..., 0, :], -values[..., 1, :]], axis=-2)


def propagate(values, spectrum, forward, inverse):
    moved_on = transform(values.astype(jnp.bfloat16), forward)
    return transform(complex_times(moved_on, spectrum).astype(jnp.bfloat16), inverse)


def propagator(wave_nums, points_all):
    counter = jnp.arange(points_all, dtype=jnp.int32)
    folded = jnp.where(counter < points_all // 2, counter, counter - points_all).astype(jnp.float32)
    lateral = 2.0 * math.pi / points_all * folded
    excess = wave_nums[:, None] ** 2 - lateral[None, :] ** 2
    upward = jnp.sqrt(jnp.maximum(excess, 0.0)) * STEP_DEPTH
    damped = jnp.sqrt(jnp.maximum(-excess, 0.0)) * STEP_DEPTH
    real_part = jnp.where(excess > 0, jnp.cos(upward), jnp.exp(-damped))
    imag_part = jnp.where(excess > 0, jnp.sin(upward), jnp.zeros_like(upward))
    return jnp.stack([real_part, imag_part], axis=1)


def screens(wave_nums, slowness):
    phase = wave_nums[:, None, None] * STEP_DEPTH * slowness[None]
    return jnp.stack([jnp.cos(phase), jnp.sin(phase)], axis=2)


def encoded_sources(incident, encode, sources):
    shifts = jnp.arange(sources, dtype=jnp.int32)
    bit_set = encode[:, None] >> shifts[None, :] & 1
    signs_all = (1 - 2 * bit_set).astype(jnp.float32)
    return jnp.sum(signs_all[:, :, None, None] * incident, axis=1)


def lookup_waves(freq_index, wavenum, table_size):
    onehot_rows = (freq_index[:, None] == jnp.arange(table_size, dtype=jnp.int32)[None, :]).astype(
        jnp.float32
    )
    return jnp.sum(onehot_rows * wavenum[None, :], axis=1)


def shards(incident, encode, freq_index, wavenum, slowness, probes):
    points_all = SIDE * SIDE
    forward = dft_tables(SIDE, -1.0)
    inverse = dft_tables(SIDE, 1.0)
    group_count = incident.shape[0]
    probe_count = probes.shape[0]
    src_count = lax.axis_size(SRC_AXES)
    depth_count = lax.axis_size("depth")
    slowness_all = lax.all_gather(slowness, "depth", axis=0, tiled=True)
    plane_count = slowness_all.shape[0]
    probe_mine = lax.all_to_all(probes, "depth", 0, 1, tiled=True).astype(jnp.float32)
    sources = encoded_sources(incident, encode, incident.shape[1])
    wave_nums = lookup_waves(freq_index, wavenum, wavenum.shape[0])
    spectra = propagator(wave_nums, points_all)
    spectra_back = conjugate(spectra)
    plane_screens = screens(wave_nums, slowness_all)
    born_scale = wave_nums * STEP_DEPTH
    fields = []
    current = sources
    for plane in range(plane_count):
        current = complex_times(
            plane_screens[:, plane], propagate(current, spectra, forward, inverse)
        )
        fields.append(current)

    def born(plane):
        scaled = born_scale[:, None, None] * probe_mine[None, :, plane]
        background = fields[plane]
        return jnp.stack(
            [-scaled * background[:, None, 1], scaled * background[:, None, 0]], axis=2
        )

    tangent = born(0)
    for plane in range(1, plane_count):
        moved_on = complex_times(
            plane_screens[:, plane][:, None], propagate(tangent, spectra[:, None], forward, inverse)
        )
        tangent = moved_on + born(plane)
    adjoint = tangent
    pieces = [None] * plane_count
    for plane in reversed(range(plane_count)):
        background = fields[plane]
        product_terms = born_scale[:, None, None] * (
            background[:, None, 0] * adjoint[:, :, 1] - background[:, None, 1] * adjoint[:, :, 0]
        )
        pieces[plane] = jnp.sum(product_terms, axis=0)
        if plane > 0:
            turned_back = complex_times(conjugate(plane_screens[:, plane])[:, None], adjoint)
            adjoint = propagate(turned_back, spectra_back[:, None], forward, inverse)
    sketch_part = jnp.stack(pieces, axis=1)
    rows, planes = (sketch_part.shape[0], sketch_part.shape[1])
    by_axes = sketch_part.reshape(rows, planes, CHIPS_Y, CHIPS_Z, CORES, -1)
    by_axes = jnp.transpose(by_axes, (4, 3, 2, 0, 1, 5))
    summed = lax.psum_scatter(by_axes, "core", scatter_dimension=0)
    summed = lax.psum_scatter(summed, "chip_z", scatter_dimension=0)
    summed = lax.psum_scatter(summed, "chip_y", scatter_dimension=0)
    summed = lax.all_gather(summed, "depth", axis=0, tiled=True)
    slab_width = summed.shape[2]
    src_index = lax.axis_index(SRC_AXES)
    local_probes = lax.dynamic_slice_in_dim(probes, src_index * slab_width, slab_width, 2)
    local_probes = lax.all_gather(local_probes, "depth", axis=1, tiled=True).astype(jnp.float32)
    sketch_all = summed / (group_count * src_count) + DAMPING * local_probes
    flattened_all = sketch_all.reshape(probe_count, -1)
    row_total = flattened_all.shape[1] * src_count
    gram_local = (
        jnp.dot(flattened_all, flattened_all.T, precision=lax.Precision.HIGHEST) / row_total
    )
    gram_matrix = lax.psum(gram_local, "core")
    gram_matrix = lax.psum(gram_matrix, "chip_z")
    gram_matrix = lax.psum(gram_matrix, "chip_y")
    sketch = lax.dynamic_slice_in_dim(sketch_all, lax.axis_index("depth"), 1, 1)
    local_planes = 1
    flattened = sketch.reshape(probe_count, local_planes * slab_width)
    lower_factor = jnp.linalg.cholesky(gram_matrix)
    identity = jnp.eye(probe_count, dtype=jnp.float32)
    inverse_lower = lax.linalg.triangular_solve(lower_factor, identity, left_side=True, lower=True)
    sketch_basis = jnp.dot(inverse_lower, flattened, precision=lax.Precision.HIGHEST).reshape(
        probe_count, local_planes, slab_width
    )
    return (sketch_basis, lower_factor.T)


def solution(mesh):
    src_size, depth_size = mesh.devices.shape
    cut = mesh.devices.reshape(CHIPS_Y, CHIPS_Z, CORES, depth_size)
    fine = Mesh(cut, SRC_AXES + ("depth",))
    in_specs = (
        P(SRC_AXES, None, None, None),
        P(SRC_AXES),
        P(SRC_AXES),
        P(),
        P("depth", None),
        P(None, "depth", None),
    )
    out_specs = (P(None, "depth", SRC_AXES), P())
    return jax.shard_map(shards, mesh=fine, in_specs=in_specs, out_specs=out_specs, check_vma=False)
```

profile of v0, /device:TPU:2, one launch (start us, length us, event | category | flops | bytes accessed | tf_op | source)
XLA Modules:
  0.0 331.6 jit_solution(9152057225294256255)
XLA Ops:
  7.7 2.0 reduce.49
  9.7 1.2 reshape.3022
  10.9 9.3 %all-to-all-start = ((bf16[4,2,32768]{2,1,0:T(2,128)(2,1)}), bf16[4,2,32768]{2,1,0:T(2,128)(2,1)S(1)}, u32[]{:S(2)}, u32[]{:S(2)}) async-start(bf16[4,2,32768]{2,1,0:T(2,128)(2,1)} %reshape.3022), calls=%async_computation | async-start | bytes 1048576 | tf_op jit(solution)/shard_map/all_to_all | solution.py:109
  21.4 1.3 fusion.124
  25.0 12.6 %all-gather.1 = f32[4,1,4096]{2,1,0:T(1,128)S(1)} all-gather(f32[1,1,4096]{2,1,0:T(1,128)} %bitcast.531), channel_id=1, replica_groups=mesh['chip_y'=8,'chip_z'=8,'core'=2,'depth'=4] {'depth'}, dimensions={0}, use_global_device_ids=true | all-gather | bytes 81920 | tf_op jit(solution)/shard_map/all_gather | solution.py:107
  37.7 2.5 cosine_bitcast_fusion
  55.3 1.2 fusion.134
  66.3 1.7 multiply_bitcast_fusion.1
  86.7 0.9 subtract_convert_fusion.15
  91.6 0.8 subtract_convert_fusion.13
  96.4 0.9 squeeze.29
  97.3 1.9 squeeze.28
  99.2 2.1 squeeze.31
  101.3 2.8 squeeze.30
  104.1 1.9 squeeze.33
  106.0 1.9 squeeze.32
  108.0 1.8 squeeze.35
  109.8 1.9 squeeze.34
  111.8 2.3 subtract_multiply_fusion.3
  114.1 2.1 subtract_multiply_fusion.2
  117.8 2.2 maximum_bitcast_fusion
  120.1 4.4 %copy.305 = f32[2,8,8,16,4,32]{5,3,4,2,1,0:T(8,128)} copy(f32[2,8,8,16,4,32]{5,0,1,2,3,4:T(2,128)S(1)} %maximum_bitcast_fusion) | data formatting | bytes 2097152 | tf_op jit(solution)/shard_map/transpose | solution.py:151
  124.5 20.2 %reduce-scatter.4.cloned.1.call-done = f32[1,8,8,16,4,32]{5,3,4,2,1,0:T(8,128)} async-done(((f32[2,8,8,16,4,32]{5,3,4,2,1,0:T(8,128)}), f32[1,8,8,16,4,32]{5,3,4,2,1,0:T(8,128)}) %reduce-scatter.4.cloned.1.call-update) | async-done | bytes 524304 | tf_op jit(solution)/shard_map/reduce_scatter | solution.py:152
  144.8 49.8 %reduce-scatter.6.cloned.1.call-done = f32[1,8,16,4,32]{4,2,3,1,0:T(8,128)} async-done(((f32[8,8,16,4,32]{4,2,3,1,0:T(8,128)}), f32[1,8,16,4,32]{4,2,3,1,0:T(8,128)}) %reduce-scatter.6.cloned.1.call-update) | async-done | bytes 65552 | tf_op jit(solution)/shard_map/reduce_scatter | solution.py:153
  195.5 12.2 %all_gather.11 = bf16[64,4,32]{0,2,1:T(8,128)(2,1)S(1)} all-gather(bf16[64,1,32]{0,2,1:T(8,128)(2,1)S(1)} %copy.373), channel_id=1, replica_groups=mesh['chip_y'=8,'chip_z'=8,'core'=2,'depth'=4] {'depth'}, dimensions={1}, use_global_device_ids=true | all-gather | bytes 20480 | tf_op jit(solution)/shard_map/all_gather | solution.py:159
  207.7 27.2 %reduce-scatter.8.cloned.1.call-done = f32[1,16,4,32]{3,1,2,0:T(8,128)} async-done(((f32[8,16,4,32]{3,1,2,0:T(8,128)}), f32[1,16,4,32]{3,1,2,0:T(8,128)}) %reduce-scatter.8.cloned.1.call-update) | async-done | bytes 8208 | tf_op jit(solution)/shard_map/reduce_scatter | solution.py:154
  235.7 12.0 %all-gather = f32[1,64,4,32]{3,2,0,1:T(4,128)S(1)} all-gather(f32[1,16,4,32]{3,2,0,1:T(4,128)S(1)} %copy.306), channel_id=2, replica_groups=mesh['chip_y'=8,'chip_z'=8,'core'=2,'depth'=4] {'depth'}, dimensions={1}, use_global_device_ids=true | all-gather | bytes 40960 | tf_op jit(solution)/shard_map/all_gather | solution.py:155
  248.1 3.4 %psum.21 = f32[64,64]{0,1:T(8,128)S(1)} all-reduce(f32[64,64]{0,1:T(8,128)S(1)} %fusion), channel_id=1, replica_groups=mesh['chip_y'=8,'chip_z'=8,'core'=2,'depth'=4] {'core'}, use_global_device_ids=true, to_apply=%region_5.6 | all-reduce | flops 4096 | bytes 32768 | tf_op jit(solution)/shard_map/psum | solution.py:166
  251.5 30.9 %psum.22 = f32[64,64]{0,1:T(8,128)S(1)} all-reduce(f32[64,64]{0,1:T(8,128)S(1)} %psum.21), channel_id=1, replica_groups=mesh['chip_y'=8,'chip_z'=8,'core'=2,'depth'=4] {'chip_z'}, use_global_device_ids=true, to_apply=%region_6.7 | all-reduce | flops 4096 | bytes 32768 | tf_op jit(solution)/shard_map/psum | solution.py:167
  282.4 28.3 %psum.23 = f32[64,64]{0,1:T(8,128)S(1)} all-reduce(f32[64,64]{0,1:T(8,128)S(1)} %psum.22), channel_id=1, replica_groups=mesh['chip_y'=8,'chip_z'=8,'core'=2,'depth'=4] {'chip_y'}, use_global_device_ids=true, to_apply=%region_7.8 | all-reduce | flops 4096 | bytes 32768 | tf_op jit(solution)/shard_map/psum | solution.py:168
  310.8 5.8 %cholesky.17 = f32[64,64]{1,0:T(8,128)S(1)} custom-call(f32[64,64]{1,0:T(8,128)S(1)} %fusion.80), custom_call_target="Cholesky" | custom-call | tf_op jit(solution)/shard_map/jit(cholesky)/cholesky | solution.py:172
  318.0 4.9 %custom-call.6 = f32[1,64,64]{1,2,0:T(8,128)S(1)} custom-call(f32[1,64,64]{2,1,0:T(8,128)S(1)} %get-tuple-element.115), custom_call_target="InvertDiagBlocksLowerTriangular" | custom-call | tf_op jit(solution)/shard_map/triangular_solve | solution.py:174
  (286 shorter events, 58.8 us)
Async XLA Ops:
  7.2 34.7 %copy-start.16 = (f32[1,4,2,4096]{3,2,1,0:T(2,128)S(1)}, f32[1,4,2,4096]{3,2,1,0:T(2,128)}, u32[]{:S(2)}) copy-start(f32[1,4,2,4096]{3,2,1,0:T(2,128)} %param.6) | copy-start | bytes 393220
  10.9 54.0 %all-to-all-start = ((bf16[4,2,32768]{2,1,0:T(2,128)(2,1)}), bf16[4,2,32768]{2,1,0:T(2,128)(2,1)S(1)}, u32[]{:S(2)}, u32[]{:S(2)}) async-start(bf16[4,2,32768]{2,1,0:T(2,128)(2,1)} %reshape.3022), calls=%async_computation | async-start | bytes 1048576 | tf_op jit(solution)/shard_map/all_to_all | solution.py:109
  20.2 124.5 %reduce-scatter.4.cloned.1.call-start = ((), (), s32[]{:S(2)}) async-start(), calls=%async_computation.4 | async-start | bytes 6291456 | tf_op jit(solution)/shard_map/reduce_scatter | solution.py:152
  45.9 20.3 %copy-start.14 = (f32[1,1,4096]{2,1,0:T(1,128)}, f32[1,1,4096]{2,1,0:T(1,128)S(1)}, u32[]{:S(2)}) copy-start(f32[1,1,4096]{2,1,0:T(1,128)S(1)} %get-tuple-element.15) | copy-start | bytes 49156
  46.0 20.3 %copy-start.15 = (f32[1,1,4096]{2,1,0:T(1,128)}, f32[1,1,4096]{2,1,0:T(1,128)S(1)}, u32[]{:S(2)}) copy-start(f32[1,1,4096]{2,1,0:T(1,128)S(1)} %get-tuple-element.111) | copy-start | bytes 49156
  49.3 17.0 %copy-start.10 = (f32[1,1,4096]{2,1,0:T(1,128)}, f32[1,1,4096]{2,1,0:T(1,128)S(1)}, u32[]{:S(2)}) copy-start(f32[1,1,4096]{2,1,0:T(1,128)S(1)} %get-tuple-element.19) | copy-start | bytes 49156
  49.3 17.0 %copy-start.11 = (f32[1,1,4096]{2,1,0:T(1,128)}, f32[1,1,4096]{2,1,0:T(1,128)S(1)}, u32[]{:S(2)}) copy-start(f32[1,1,4096]{2,1,0:T(1,128)S(1)} %get-tuple-element.107) | copy-start | bytes 49156
  52.6 13.7 %copy-start.12 = (f32[1,1,4096]{2,1,0:T(1,128)}, f32[1,1,4096]{2,1,0:T(1,128)S(1)}, u32[]{:S(2)}) copy-start(f32[1,1,4096]{2,1,0:T(1,128)S(1)} %get-tuple-element.23) | copy-start | bytes 49156
  52.6 13.7 %copy-start.13 = (f32[1,1,4096]{2,1,0:T(1,128)}, f32[1,1,4096]{2,1,0:T(1,128)S(1)}, u32[]{:S(2)}) copy-start(f32[1,1,4096]{2,1,0:T(1,128)S(1)} %get-tuple-element.105) | copy-start | bytes 49156
  79.5 2.1 copy-start.17
  79.5 2.1 copy-start.18
  80.3 1.5 copy-start.23
  80.3 1.5 copy-start.24
  82.5 2.1 copy-start.9
  84.7 2.0 copy-start.21
  84.7 2.0 copy-start.22
  89.5 2.0 copy-start.19
  89.5 2.0 copy-start.20
  96.4 7.8 %copy-start.4 = (f32[1,16,1,4096]{3,1,2,0:T(8,128)S(1)}, f32[1,16,1,4096]{3,1,2,0:T(8,128)}, u32[]{:S(2)}) copy-start(f32[1,16,1,4096]{3,1,2,0:T(8,128)} %get-tuple-element.89) | copy-start | bytes 786436
  96.4 9.7 %copy-start.3 = (f32[1,16,1,4096]{3,1,2,0:T(8,128)S(1)}, f32[1,16,1,4096]{3,1,2,0:T(8,128)}, u32[]{:S(2)}) copy-start(f32[1,16,1,4096]{3,1,2,0:T(8,128)} %get-tuple-element.88) | copy-start | bytes 786436
  99.2 12.5 %copy-start.5 = (f32[8,8,2,32]{3,2,1,0:T(2,128)S(1)}, f32[8,8,2,32]{3,2,1,0:T(2,128)}, u32[]{:S(2)}) copy-start(f32[8,8,2,32]{3,2,1,0:T(2,128)} %mul.2738) | copy-start | bytes 49156
  111.7 4.4 %copy-start = (f32[16,1,8,8,2,32]{5,4,3,2,0,1:T(2,128)S(1)}, f32[16,1,8,8,2,32]{5,4,3,2,0,1:T(2,128)}, u32[]{:S(2)}) copy-start(f32[16,1,8,8,2,32]{5,4,3,2,0,1:T(2,128)} %squeeze.33) | copy-start | bytes 786436
  111.7 4.5 %copy-start.2 = (f32[16,1,8,8,2,32]{5,4,3,2,0,1:T(2,128)S(1)}, f32[16,1,8,8,2,32]{5,4,3,2,0,1:T(2,128)}, u32[]{:S(2)}) copy-start(f32[16,1,8,8,2,32]{5,4,3,2,0,1:T(2,128)} %squeeze.32) | copy-start | bytes 786436
  111.7 4.5 %copy-start.6 = (f32[8,8,2,32]{3,2,1,0:T(2,128)S(1)}, f32[8,8,2,32]{3,2,1,0:T(2,128)}, u32[]{:S(2)}) copy-start(f32[8,8,2,32]{3,2,1,0:T(2,128)} %mul.2752) | copy-start | bytes 49156
  111.7 4.5 %copy-start.8 = (f32[8,8,2,32]{3,2,1,0:T(2,128)S(1)}, f32[8,8,2,32]{3,2,1,0:T(2,128)}, u32[]{:S(2)}) copy-start(f32[8,8,2,32]{3,2,1,0:T(2,128)} %mul.2749) | copy-start | bytes 49156
  111.7 5.3 %copy-start.1 = (f32[16,1,8,8,2,32]{5,4,3,2,0,1:T(2,128)S(1)}, f32[16,1,8,8,2,32]{5,4,3,2,0,1:T(2,128)}, u32[]{:S(2)}) copy-start(f32[16,1,8,8,2,32]{5,4,3,2,0,1:T(2,128)} %squeeze.34) | copy-start | bytes 786436
  111.7 5.3 %copy-start.7 = (f32[8,8,2,32]{3,2,1,0:T(2,128)S(1)}, f32[8,8,2,32]{3,2,1,0:T(2,128)}, u32[]{:S(2)}) copy-start(f32[8,8,2,32]{3,2,1,0:T(2,128)} %mul.2756) | copy-start | bytes 49156
  124.5 70.1 %reduce-scatter.6.cloned.1.call-start = ((), (), s32[]{:S(2)}) async-start(), calls=%async_computation.5 | async-start | bytes 2359296 | tf_op jit(solution)/shard_map/reduce_scatter | solution.py:153
  144.7 90.2 %reduce-scatter.8.cloned.1.call-start = ((), (), s32[]{:S(2)}) async-start(), calls=%async_computation.6 | async-start | bytes 294912 | tf_op jit(solution)/shard_map/reduce_scatter | solution.py:154
Sparse Core Ops, SparseCore 0:
  124.6 20.0 reduce-scatter.3
  147.8 46.7 reduce-scatter.5
  197.6 37.2 reduce-scatter.7
where the time goes:
time: 335 us; the launch traced here: 332 us
  blocking collectives  99.4 us (30%)
  waiting for transfers between devices  97.2 us (29%)
  local copies, waits for them, and re-layouts  49 us (15%)
  other arithmetic  46.4 us (14%)
  between operations  18.1 us (5%)
  matrix products  12 us (4%)
  starting transfers between devices  9.43 us (3%)
    reduce_scatter x1, waiting for transfers between devices, shards(): summed = lax.psum_scatter(summed, 'chip_z', scatter_dimension=0)  49.8 us
    psum x1, blocking collectives, shards(): gram_matrix = lax.psum(gram_matrix, 'chip_z')  30.9 us
    psum x1, blocking collectives, shards(): gram_matrix = lax.psum(gram_matrix, 'chip_y')  28.3 us
    reduce_scatter x1, waiting for transfers between devices, shards(): summed = lax.psum_scatter(summed, 'chip_y', scatter_dimension=0)  27.2 us
    reduce_scatter x1, waiting for transfers between devices, shards(): summed = lax.psum_scatter(by_axes, 'core', scatter_dimension=0)  20.2 us
    all_gather x1, blocking collectives, shards(): slowness_all = lax.all_gather(slowness, 'depth', axis=0, tiled=True)  12.6 us
    all_gather x1, blocking collectives, shards(): lax.all_gather(local_probes, 'depth', axis=1, tiled=True)  12.2 us
    all_gather x1, blocking collectives, shards(): summed = lax.all_gather(summed, 'depth', axis=0, tiled=True)  12 us
  transfers between devices with their start and end apart: 4, of which 3 were waited for; matrix products, arithmetic and copies ran while one was open for 9% of the time, Pallas kernels for 0%

commit v1 on v0

--- a/solution.py
+++ b/solution.py
@@ -106,7 +106,15 @@
     depth_count = lax.axis_size("depth")
     slowness_all = lax.all_gather(slowness, "depth", axis=0, tiled=True)
     plane_count = slowness_all.shape[0]
-    probe_mine = lax.all_to_all(probes, "depth", 0, 1, tiled=True).astype(jnp.float32)
+    probe_mine = jnp.concatenate(
+        jax.lax.all_to_all(
+            jnp.stack(jnp.split(probes, jax.lax.axis_size("depth"), 0), axis=0),
+            "depth",
+            split_axis=0,
+            concat_axis=0,
+        ),
+        1,
+    ).astype(jnp.float32)
     sources = encoded_sources(incident, encode, incident.shape[1])
     wave_nums = lookup_waves(freq_index, wavenum, wavenum.shape[0])
     spectra = propagator(wave_nums, points_all)

time: 335 us -> 331 us (0.988)
    another operation x30 -> x31, other arithmetic: 7.19 us -> 8.04 us
where the time goes in v1:
time: 331 us; the launch traced here: 327 us
  blocking collectives  98.5 us (30%)
  waiting for transfers between devices  97.6 us (29%)
  local copies, waits for them, and re-layouts  47 us (14%)
  other arithmetic  44.6 us (13%)
  between operations  17.7 us (5%)
  matrix products  12 us (4%)
  starting transfers between devices  9.43 us (3%)
    reduce_scatter x1, waiting for transfers between devices, shards(): summed = lax.psum_scatter(summed, 'chip_z', scatter_dimension=0)  50.1 us
    psum x1, blocking collectives, shards(): gram_matrix = lax.psum(gram_matrix, 'chip_z')  30.8 us
    psum x1, blocking collectives, shards(): gram_matrix = lax.psum(gram_matrix, 'chip_y')  28.4 us
    reduce_scatter x1, waiting for transfers between devices, shards(): summed = lax.psum_scatter(summed, 'chip_y', scatter_dimension=0)  27.3 us
    reduce_scatter x1, waiting for transfers between devices, shards(): summed = lax.psum_scatter(by_axes, 'core', scatter_dimension=0)  20.2 us
    all_gather x1, blocking collectives, shards(): slowness_all = lax.all_gather(slowness, 'depth', axis=0, tiled=True)  12.1 us
    all_gather x1, blocking collectives, shards(): summed = lax.all_gather(summed, 'depth', axis=0, tiled=True)  12 us
    all_gather x1, blocking collectives, shards(): lax.all_gather(local_probes, 'depth', axis=1, tiled=True)  11.8 us
  transfers between devices with their start and end apart: 4, of which 3 were waited for; matrix products, arithmetic and copies ran while one was open for 9% of the time, Pallas kernels for 0%

profile of v1, /device:TPU:2, one launch (start us, length us, event | category | flops | bytes accessed | tf_op | source)
XLA Modules:
  0.0 327.0 jit_solution(7855665159407990239)
XLA Ops:
  7.2 1.2 slice_bitcast_fusion.3
  8.3 0.9 pad_maximum_fusion
  9.2 9.3 %all-to-all-start = ((bf16[4,16,1,4096]{3,1,2,0:T(8,128)(2,1)}), bf16[4,16,1,4096]{3,1,2,0:T(8,128)(2,1)S(1)}, u32[]{:S(2)}, u32[]{:S(2)}) async-start(bf16[4,16,1,4096]{3,1,2,0:T(8,128)(2,1)} %pad_maximum_fusion), calls=%async_computation | async-start | bytes 1048576 | tf_op jit(solution)/shard_map/all_to_all | solution.py:110
  19.7 1.3 fusion.124
  23.2 12.1 %all-gather.1 = f32[4,1,4096]{2,1,0:T(1,128)S(1)} all-gather(f32[1,1,4096]{2,1,0:T(1,128)} %bitcast.534), channel_id=1, replica_groups=mesh['chip_y'=8,'chip_z'=8,'core'=2,'depth'=4] {'depth'}, dimensions={0}, use_global_device_ids=true | all-gather | bytes 81920 | tf_op jit(solution)/shard_map/all_gather | solution.py:107
  35.3 3.0 cosine_bitcast_fusion
  67.5 0.8 multiply_subtract_fusion.2
  82.3 0.9 subtract_convert_fusion.15
  87.3 0.8 subtract_convert_fusion.13
  92.2 0.9 squeeze.29
  93.1 1.9 squeeze.28
  95.0 1.9 squeeze.31
  96.8 2.8 squeeze.30
  99.7 1.9 squeeze.33
  101.5 1.9 squeeze.32
  103.5 1.8 squeeze.35
  105.3 1.9 squeeze.34
  107.3 2.6 subtract_multiply_fusion.3
  109.9 2.0 subtract_multiply_fusion.2
  113.4 2.2 maximum_bitcast_fusion
  115.7 4.4 %copy.301 = f32[2,8,8,16,4,32]{5,3,4,2,1,0:T(8,128)} copy(f32[2,8,8,16,4,32]{5,0,1,2,3,4:T(2,128)S(1)} %maximum_bitcast_fusion) | data formatting | bytes 2097152 | tf_op jit(solution)/shard_map/transpose | solution.py:159
  120.1 20.2 %reduce-scatter.4.cloned.1.call-done = f32[1,8,8,16,4,32]{5,3,4,2,1,0:T(8,128)} async-done(((f32[2,8,8,16,4,32]{5,3,4,2,1,0:T(8,128)}), f32[1,8,8,16,4,32]{5,3,4,2,1,0:T(8,128)}) %reduce-scatter.4.cloned.1.call-update) | async-done | bytes 524304 | tf_op jit(solution)/shard_map/reduce_scatter | solution.py:160
  140.4 50.1 %reduce-scatter.6.cloned.1.call-done = f32[1,8,16,4,32]{4,2,3,1,0:T(8,128)} async-done(((f32[8,8,16,4,32]{4,2,3,1,0:T(8,128)}), f32[1,8,16,4,32]{4,2,3,1,0:T(8,128)}) %reduce-scatter.6.cloned.1.call-update) | async-done | bytes 65552 | tf_op jit(solution)/shard_map/reduce_scatter | solution.py:161
  190.5 0.8 constant_dynamic-slice_fusion
  191.4 11.8 %all_gather.11 = bf16[64,4,32]{0,2,1:T(8,128)(2,1)S(1)} all-gather(bf16[64,1,32]{0,2,1:T(8,128)(2,1)S(1)} %copy.369), channel_id=1, replica_groups=mesh['chip_y'=8,'chip_z'=8,'core'=2,'depth'=4] {'depth'}, dimensions={1}, use_global_device_ids=true | all-gather | bytes 20480 | tf_op jit(solution)/shard_map/all_gather | solution.py:167
  203.2 27.3 %reduce-scatter.8.cloned.1.call-done = f32[1,16,4,32]{3,1,2,0:T(8,128)} async-done(((f32[8,16,4,32]{3,1,2,0:T(8,128)}), f32[1,16,4,32]{3,1,2,0:T(8,128)}) %reduce-scatter.8.cloned.1.call-update) | async-done | bytes 8208 | tf_op jit(solution)/shard_map/reduce_scatter | solution.py:162
  231.3 12.0 %all-gather = f32[1,64,4,32]{3,2,0,1:T(4,128)S(1)} all-gather(f32[1,16,4,32]{3,2,0,1:T(4,128)S(1)} %copy.302), channel_id=2, replica_groups=mesh['chip_y'=8,'chip_z'=8,'core'=2,'depth'=4] {'depth'}, dimensions={1}, use_global_device_ids=true | all-gather | bytes 40960 | tf_op jit(solution)/shard_map/all_gather | solution.py:163
  243.7 3.4 %psum.21 = f32[64,64]{0,1:T(8,128)S(1)} all-reduce(f32[64,64]{0,1:T(8,128)S(1)} %fusion), channel_id=1, replica_groups=mesh['chip_y'=8,'chip_z'=8,'core'=2,'depth'=4] {'core'}, use_global_device_ids=true, to_apply=%region_5.6 | all-reduce | flops 4096 | bytes 32768 | tf_op jit(solution)/shard_map/psum | solution.py:174
  247.1 30.8 %psum.22 = f32[64,64]{0,1:T(8,128)S(1)} all-reduce(f32[64,64]{0,1:T(8,128)S(1)} %psum.21), channel_id=1, replica_groups=mesh['chip_y'=8,'chip_z'=8,'core'=2,'depth'=4] {'chip_z'}, use_global_device_ids=true, to_apply=%region_6.7 | all-reduce | flops 4096 | bytes 32768 | tf_op jit(solution)/shard_map/psum | solution.py:175
  277.9 28.4 %psum.23 = f32[64,64]{0,1:T(8,128)S(1)} all-reduce(f32[64,64]{0,1:T(8,128)S(1)} %psum.22), channel_id=1, replica_groups=mesh['chip_y'=8,'chip_z'=8,'core'=2,'depth'=4] {'chip_y'}, use_global_device_ids=true, to_apply=%region_7.8 | all-reduce | flops 4096 | bytes 32768 | tf_op jit(solution)/shard_map/psum | solution.py:176
  306.4 5.8 %cholesky.17 = f32[64,64]{1,0:T(8,128)S(1)} custom-call(f32[64,64]{1,0:T(8,128)S(1)} %fusion.80), custom_call_target="Cholesky" | custom-call | tf_op jit(solution)/shard_map/jit(cholesky)/cholesky | solution.py:180
  313.6 4.9 %custom-call.6 = f32[1,64,64]{1,2,0:T(8,128)S(1)} custom-call(f32[1,64,64]{2,1,0:T(8,128)S(1)} %get-tuple-element.119), custom_call_target="InvertDiagBlocksLowerTriangular" | custom-call | tf_op jit(solution)/shard_map/triangular_solve | solution.py:182
  (272 shorter events, 57.3 us)
Async XLA Ops:
  7.2 32.8 %copy-start.10 = (f32[1,4,2,4096]{3,2,1,0:T(2,128)S(1)}, f32[1,4,2,4096]{3,2,1,0:T(2,128)}, u32[]{:S(2)}) copy-start(f32[1,4,2,4096]{3,2,1,0:T(2,128)} %param.6) | copy-start | bytes 393220
  9.2 53.5 %all-to-all-start = ((bf16[4,16,1,4096]{3,1,2,0:T(8,128)(2,1)}), bf16[4,16,1,4096]{3,1,2,0:T(8,128)(2,1)S(1)}, u32[]{:S(2)}, u32[]{:S(2)}) async-start(bf16[4,16,1,4096]{3,1,2,0:T(8,128)(2,1)} %pad_maximum_fusion), calls=%async_computation | async-start | bytes 1048576 | tf_op jit(solution)/shard_map/all_to_all | solution.py:110
  18.5 121.8 %reduce-scatter.4.cloned.1.call-start = ((), (), s32[]{:S(2)}) async-start(), calls=%async_computation.4 | async-start | bytes 6291456 | tf_op jit(solution)/shard_map/reduce_scatter | solution.py:160
  75.3 2.1 copy-start.11
  75.3 2.1 copy-start.12
  76.0 1.5 copy-start.17
  76.0 1.5 copy-start.18
  78.2 1.9 copy-start.9
  80.2 2.0 copy-start.15
  80.2 2.0 copy-start.16
  85.3 2.0 copy-start.13
  85.3 2.0 copy-start.14
  92.1 7.5 %copy-start.4 = (f32[1,16,1,4096]{3,1,2,0:T(8,128)S(1)}, f32[1,16,1,4096]{3,1,2,0:T(8,128)}, u32[]{:S(2)}) copy-start(f32[1,16,1,4096]{3,1,2,0:T(8,128)} %get-tuple-element.89) | copy-start | bytes 786436
  92.1 9.4 %copy-start.3 = (f32[1,16,1,4096]{3,1,2,0:T(8,128)S(1)}, f32[1,16,1,4096]{3,1,2,0:T(8,128)}, u32[]{:S(2)}) copy-start(f32[1,16,1,4096]{3,1,2,0:T(8,128)} %get-tuple-element.88) | copy-start | bytes 786436
  95.0 12.3 %copy-start.5 = (f32[8,8,2,32]{3,2,1,0:T(2,128)S(1)}, f32[8,8,2,32]{3,2,1,0:T(2,128)}, u32[]{:S(2)}) copy-start(f32[8,8,2,32]{3,2,1,0:T(2,128)} %mul.2738) | copy-start | bytes 49156
  107.2 4.6 %copy-start = (f32[16,1,8,8,2,32]{5,4,3,2,0,1:T(2,128)S(1)}, f32[16,1,8,8,2,32]{5,4,3,2,0,1:T(2,128)}, u32[]{:S(2)}) copy-start(f32[16,1,8,8,2,32]{5,4,3,2,0,1:T(2,128)} %squeeze.33) | copy-start | bytes 786436
  107.2 4.6 %copy-start.2 = (f32[16,1,8,8,2,32]{5,4,3,2,0,1:T(2,128)S(1)}, f32[16,1,8,8,2,32]{5,4,3,2,0,1:T(2,128)}, u32[]{:S(2)}) copy-start(f32[16,1,8,8,2,32]{5,4,3,2,0,1:T(2,128)} %squeeze.32) | copy-start | bytes 786436
  107.2 4.7 %copy-start.6 = (f32[8,8,2,32]{3,2,1,0:T(2,128)S(1)}, f32[8,8,2,32]{3,2,1,0:T(2,128)}, u32[]{:S(2)}) copy-start(f32[8,8,2,32]{3,2,1,0:T(2,128)} %mul.2752) | copy-start | bytes 49156
  107.2 4.7 %copy-start.8 = (f32[8,8,2,32]{3,2,1,0:T(2,128)S(1)}, f32[8,8,2,32]{3,2,1,0:T(2,128)}, u32[]{:S(2)}) copy-start(f32[8,8,2,32]{3,2,1,0:T(2,128)} %mul.2749) | copy-start | bytes 49156
  107.2 5.4 %copy-start.1 = (f32[16,1,8,8,2,32]{5,4,3,2,0,1:T(2,128)S(1)}, f32[16,1,8,8,2,32]{5,4,3,2,0,1:T(2,128)}, u32[]{:S(2)}) copy-start(f32[16,1,8,8,2,32]{5,4,3,2,0,1:T(2,128)} %squeeze.34) | copy-start | bytes 786436
  107.3 5.4 %copy-start.7 = (f32[8,8,2,32]{3,2,1,0:T(2,128)S(1)}, f32[8,8,2,32]{3,2,1,0:T(2,128)}, u32[]{:S(2)}) copy-start(f32[8,8,2,32]{3,2,1,0:T(2,128)} %mul.2756) | copy-start | bytes 49156
  120.1 70.4 %reduce-scatter.6.cloned.1.call-start = ((), (), s32[]{:S(2)}) async-start(), calls=%async_computation.5 | async-start | bytes 2359296 | tf_op jit(solution)/shard_map/reduce_scatter | solution.py:161
  140.3 90.2 %reduce-scatter.8.cloned.1.call-start = ((), (), s32[]{:S(2)}) async-start(), calls=%async_computation.6 | async-start | bytes 294912 | tf_op jit(solution)/shard_map/reduce_scatter | solution.py:162
Sparse Core Ops, SparseCore 0:
  120.2 20.0 reduce-scatter.3
  143.4 47.0 reduce-scatter.5
  193.5 36.9 reduce-scatter.7
